TPU v7x, 32 devices: a whole 2x2x4 slice. The times are simulated.
32 devices in a mesh: tm: 8 (over z, x), slab: 4 (over y, core).
Axes of the slice: x: 2, y: 2, z: 4, core: 2. Of those that a mesh axis runs over, the one named last changes fastest.
Arguments:
- source: float32 [32, 256, 2048], P('tm', 'slab'), may hold values from -6 to 6
- guess: float32 [32, 256, 2048], P('tm', 'slab'), may hold values from -2.5 to 2.5
- field: float32 [32, 256, 2048], P('tm', 'slab'), may hold values from -2.5 to 2.5
Outputs:
- solution: float32 [32, 256, 2048], P('tm', 'slab')
- residual_new: float32 [32, 256, 2048], P('tm', 'slab')
- force: float32 [32, 256, 2048], P('tm', 'slab')
All inputs are finite; a program needn't handle non-finite values.
Results may differ from a plain program's by a relative error of at most 0.000021.
Values sent between devices are 32-bit elements; how exact they have to be, the bound alone decides.
A program may use at most 64 MiB of HBM per device.

v0:
```python
import jax
import jax.numpy as jnp
from jax import lax
from jax.sharding import PartitionSpec as P

HOP_WEIGHT = 0.125
BOSON_WEIGHT = 2.0


def padded_2(x, sides, width):
    for axis, dim in sides:
        count, length = (lax.axis_size(axis), x.shape[dim])
        up = [(i, (i + 1) % count) for i in range(count - 1)]
        down = [(j, i) for i, j in up]
        last = lax.slice_in_dim(x, length - width, length, axis=dim)
        leading = lax.slice_in_dim(x, 0, width, axis=dim)
        before = lax.ppermute(last, axis, up)
        after = lax.ppermute(leading, axis, down)
        x = jnp.concatenate([before, x, after], axis=dim)
    return x


def from_behind(x, axis, by):
    count = lax.axis_size(axis)
    return lax.ppermute(x, axis, [(i, (i + by) % count) for i in range(count)])


def hopping(padded, parity_even):
    center = padded[:, 1:-1, :]
    sideways = jnp.roll(center, 1, axis=2) + jnp.roll(center, -1, axis=2)
    vertical = jnp.where(parity_even, padded[:, 2:, :], padded[:, :-2, :])
    return center + HOP_WEIGHT * (sideways + vertical)


def on_device(source, guess, field):
    slice_count, row_count, column_count = source.shape
    slices_all = lax.axis_size("tm") * slice_count
    slice_ids = lax.axis_index("tm") * slice_count + jnp.arange(slice_count, dtype=jnp.int32)
    row_ids = lax.axis_index("slab") * row_count + jnp.arange(row_count, dtype=jnp.int32)[:, None]
    column_ids = jnp.arange(column_count, dtype=jnp.int32)[None, :]
    parity_even = ((row_ids + column_ids) % 2 == 0)[None]
    sign_here = jnp.where(slice_ids == 0, -1.0, 1.0).astype(jnp.float32)[:, None, None]
    sign_after = jnp.where(slice_ids == slices_all - 1, -1.0, 1.0).astype(jnp.float32)[
        :, None, None
    ]
    weights = jnp.exp(field)

    def kinetic(values):
        padded = padded_2(values, (("slab", 1),), 1)
        return hopping(padded, parity_even)

    def forward(values):
        hopped = kinetic(values)
        carried = weights * hopped
        incoming = from_behind(carried[-1:], "tm", 1)
        image = values - sign_here * jnp.concatenate([incoming, carried[:-1]], axis=0)
        following = from_behind(image[:1], "tm", -1)
        back = weights * sign_after * jnp.concatenate([image[1:], following], axis=0)
        return (image, back, hopped)

    def normal(values):
        image, back, hopped = forward(values)
        return (image - kinetic(back), image, back, hopped)

    first_image, unused_image, guess_back, guess_hopped = normal(guess)
    residual = source - first_image
    norm_sq = lax.psum(jnp.sum(residual * residual), ("tm", "slab"))
    applied, image, resid_back, resid_hopped = normal(residual)
    curvature = lax.psum(jnp.sum(residual * applied), ("tm", "slab"))
    alpha = norm_sq / curvature
    solution = guess + alpha * residual
    residual_new = residual - alpha * applied
    back = guess_back + alpha * resid_back
    hopped = guess_hopped + alpha * resid_hopped
    force = BOSON_WEIGHT * field + 2.0 * back * hopped
    return (solution, residual_new, force)


def solution(mesh):
    in_specs = (P("tm", "slab", None), P("tm", "slab", None), P("tm", "slab", None))
    out_specs = (P("tm", "slab", None), P("tm", "slab", None), P("tm", "slab", None))
    return jax.shard_map(
        on_device, mesh=mesh, in_specs=in_specs, out_specs=out_specs, check_vma=False
    )
```

profile of v0, /device:TPU:0, one launch (start us, length us, event | category | flops | bytes accessed | tf_op | source)
XLA Modules:
  0.0 162.1 jit_solution(16196004821972446914)
XLA Ops:
  1.7 1.3 collective-permute-start
  3.0 3.0 %collective-permute-start.1 = (f32[4,1,2048]{2,1,0:T(1,128)S(1)}, f32[4,1,2048]{2,1,0:T(1,128)S(1)}, u32[]{:S(2)}, u32[]{:S(2)}) collective-permute-start(f32[4,1,2048]{2,1,0:T(1,128)S(1)} %get-tuple-element.37), channel_id=1, source_target_pairs={{0,1},{1,2},{2,3},{4,5},{5,6},{6,7},{8,9},{9,10},{10,11},{12,13},{... | collective-permute-start | bytes 98312 | tf_op jit(solution)/shard_map/ppermute | solution.py:17
  6.1 5.1 %fusion.39 = (f32[4,64,2047]{2,1,0:T(8,128)}, f32[4,64,2047]{2,1,0:T(8,128)}) fusion(f32[4,64,2048]{2,1,0:T(8,128)} %param.4), kind=kLoop, calls=%fused_computation.66 | loop fusion | bytes 8384512 | tf_op jit(solution)/shard_map/jit(_roll_static)/slice | solution.py:30
  11.6 4.5 %exponential_multiply_fusion.1 = (f32[4,64,2048]{2,1,0:T(8,128)S(1)}, f32[4,64,2048]{2,1,0:T(8,128)}) fusion(f32[4,64,2048]{2,1,0:T(8,128)} %param.5, f32[4,64,2048]{2,1,0:T(8,128)S(1)} %copy-done, f32[4,1,2048]{2,1,0:T(1,128)S(1)} %collective-permute-done.1, f32[4,1,2048]{2,1,0:T(1,128)S(1)} %collective-permute-done, pred[64,2048]{1,0:T(8,128)(4,1)S(1)} %fusion.22, ...), kind=kLoop, calls=%fused_computation.43 | loop fusion | flops 5242880 | bytes 12779520 | tf_op jit(solution)/shard_map/mul | solution.py:54
  16.2 1.3 copy-done.4
  17.5 3.0 %collective-permute-start.2 = (f32[1,64,2048]{2,1,0:T(8,128)S(1)}, f32[1,64,2048]{2,1,0:T(8,128)S(1)}, u32[]{:S(2)}, u32[]{:S(2)}) collective-permute-start(f32[1,64,2048]{2,1,0:T(8,128)S(1)} %slice.172), channel_id=1, source_target_pairs={{0,4},{4,8},{8,12},{12,16},{16,20},{20,24},{24,28},{28,0},{1,5},{5... | collective-permute-start | bytes 1572872 | tf_op jit(solution)/shard_map/ppermute | solution.py:25
  20.6 1.5 slice.173
  22.1 13.8 %collective-permute-done.2 = f32[1,64,2048]{2,1,0:T(8,128)S(1)} collective-permute-done((f32[1,64,2048]{2,1,0:T(8,128)S(1)}, f32[1,64,2048]{2,1,0:T(8,128)S(1)}, u32[]{:S(2)}, u32[]{:S(2)}) %collective-permute-start.2) | collective-permute-done | bytes 524320 | tf_op jit(solution)/shard_map/ppermute | solution.py:25
  36.4 2.4 %collective-permute-start.3 = (f32[1,64,2048]{2,1,0:T(8,128)S(1)}, f32[1,64,2048]{2,1,0:T(8,128)S(1)}, u32[]{:S(2)}, u32[]{:S(2)}) collective-permute-start(f32[1,64,2048]{2,1,0:T(8,128)S(1)} %slice.175), channel_id=1, source_target_pairs={{0,28},{4,0},{8,4},{12,8},{16,12},{20,16},{24,20},{28,24},{1,29},{... | collective-permute-start | bytes 1572872 | tf_op jit(solution)/shard_map/ppermute | solution.py:25
  38.9 11.7 %collective-permute-done.3 = f32[1,64,2048]{2,1,0:T(8,128)S(1)} collective-permute-done((f32[1,64,2048]{2,1,0:T(8,128)S(1)}, f32[1,64,2048]{2,1,0:T(8,128)S(1)}, u32[]{:S(2)}, u32[]{:S(2)}) %collective-permute-start.3) | collective-permute-done | bytes 524320 | tf_op jit(solution)/shard_map/ppermute | solution.py:25
  51.8 1.4 collective-permute-start.4
  53.2 3.0 %collective-permute-start.5 = (f32[4,1,2048]{2,1,0:T(1,128)S(1)}, f32[4,1,2048]{2,1,0:T(1,128)S(1)}, u32[]{:S(2)}, u32[]{:S(2)}) collective-permute-start(f32[4,1,2048]{2,1,0:T(1,128)S(1)} %get-tuple-element.31), channel_id=1, source_target_pairs={{0,1},{1,2},{2,3},{4,5},{5,6},{6,7},{8,9},{9,10},{10,11},{12,13},{... | collective-permute-start | bytes 98312 | tf_op jit(solution)/shard_map/ppermute | solution.py:17
  57.1 1.2 fusion.14
  59.1 1.3 collective-permute-start.6
  60.4 3.3 %collective-permute-start.7 = (f32[4,1,2048]{2,1,0:T(1,128)S(1)}, f32[4,1,2048]{2,1,0:T(1,128)S(1)}, u32[]{:S(2)}, u32[]{:S(2)}) collective-permute-start(f32[4,1,2048]{2,1,0:T(1,128)S(1)} %get-tuple-element.25), channel_id=1, source_target_pairs={{0,1},{1,2},{2,3},{4,5},{5,6},{6,7},{8,9},{9,10},{10,11},{12,13},{... | collective-permute-start | bytes 98312 | tf_op jit(solution)/shard_map/ppermute | solution.py:17
  64.6 2.7 %exponential_multiply_fusion = (f32[4,64,2048]{2,1,0:T(8,128)S(1)}, f32[4,64,2048]{2,1,0:T(8,128)}) fusion(f32[4,64,2048]{2,1,0:T(8,128)S(1)} %copy-done.3, f32[4,64,2048]{2,1,0:T(8,128)S(1)} %fusion.14, f32[4,1,2048]{2,1,0:T(1,128)S(1)} %collective-permute-done.7, f32[4,1,2048]{2,1,0:T(1,128)S(1)} %collective-permute-done.6, ...), kind=kLoop, calls=%fused_computation.42 | loop fusion | flops 5242880 | bytes 12779520 | tf_op jit(solution)/shard_map/mul | solution.py:54
  67.5 15.6 %collective-permute-done.8 = f32[1,64,2048]{2,1,0:T(8,128)S(1)} collective-permute-done((f32[1,64,2048]{2,1,0:T(8,128)S(1)}, f32[1,64,2048]{2,1,0:T(8,128)S(1)}, u32[]{:S(2)}, u32[]{:S(2)}) %collective-permute-start.8) | collective-permute-done | bytes 524320 | tf_op jit(solution)/shard_map/ppermute | solution.py:25
  83.6 2.3 %collective-permute-start.9 = (f32[1,64,2048]{2,1,0:T(8,128)S(1)}, f32[1,64,2048]{2,1,0:T(8,128)S(1)}, u32[]{:S(2)}, u32[]{:S(2)}) collective-permute-start(f32[1,64,2048]{2,1,0:T(8,128)S(1)} %slice.191), channel_id=1, source_target_pairs={{0,28},{4,0},{8,4},{12,8},{16,12},{20,16},{24,20},{28,24},{1,29},{... | collective-permute-start | bytes 1572872 | tf_op jit(solution)/shard_map/ppermute | solution.py:25
  86.0 11.8 %collective-permute-done.9 = f32[1,64,2048]{2,1,0:T(8,128)S(1)} collective-permute-done((f32[1,64,2048]{2,1,0:T(8,128)S(1)}, f32[1,64,2048]{2,1,0:T(8,128)S(1)}, u32[]{:S(2)}, u32[]{:S(2)}) %collective-permute-start.9) | collective-permute-done | bytes 524320 | tf_op jit(solution)/shard_map/ppermute | solution.py:25
  99.1 1.3 collective-permute-start.10
  100.4 3.0 %collective-permute-start.11 = (f32[4,1,2048]{2,1,0:T(1,128)S(1)}, f32[4,1,2048]{2,1,0:T(1,128)S(1)}, u32[]{:S(2)}, u32[]{:S(2)}) collective-permute-start(f32[4,1,2048]{2,1,0:T(1,128)S(1)} %get-tuple-element.19), channel_id=1, source_target_pairs={{0,1},{1,2},{2,3},{4,5},{5,6},{6,7},{8,9},{9,10},{10,11},{12,13},{... | collective-permute-start | bytes 98312 | tf_op jit(solution)/shard_map/ppermute | solution.py:17
  104.3 3.5 %multiply_reduce_fusion = (f32[]{:T(128)}, f32[]{:T(128)}, f32[4,64,2048]{2,1,0:T(8,128)}) fusion(f32[4,64,2048]{2,1,0:T(8,128)S(1)} %fusion.14, f32[4,64,2048]{2,1,0:T(8,128)S(1)} %fusion.20, f32[4,64,2048]{2,1,0:T(8,128)S(1)} %maximum_multiply_fusion.3, f32[4,1,2048]{2,1,0:T(1,128)S(1)} %collective-permute-done.11, ...), kind=kLoop, calls=%fused_computation.40 | loop fusion | flops 7340030 | bytes 12779528 | tf_op jit(solution)/shard_map/reduce_sum | solution.py:69
  107.7 43.2 %all-reduce = (f32[]{:T(128)}, f32[]{:T(128)}) all-reduce(f32[]{:T(128)} %get-tuple-element.4, f32[]{:T(128)} %get-tuple-element.3), channel_id=1, replica_groups=mesh['tm'=8,'slab'=4] {'tm','slab'}, use_global_device_ids=true, to_apply=%region_1.2 | all-reduce | flops 2 | bytes 16 | tf_op jit(solution)/shard_map/psum | solution.py:67
  152.3 9.8 %multiply_subtract_fusion = (f32[4,64,2048]{2,1,0:T(8,128)}, f32[4,64,2048]{2,1,0:T(8,128)}, f32[4,64,2048]{2,1,0:T(8,128)}) fusion(f32[4,64,2048]{2,1,0:T(8,128)S(1)} %fusion.14, f32[4,64,2048]{2,1,0:T(8,128)} %get-tuple-element.7, f32[]{:T(128)S(6)} %div.3, f32[4,64,2048]{2,1,0:T(8,128)} %param.4, f32[4,64,2048]{2,1,0:T(8,128)} %get-tuple-element.11, ...), kind=kLoop, calls=%fused_computation.38 | loop fusion | flops 6291456 | bytes 23068676 | tf_op jit(solution)/shard_map/sub | solution.py:72
  (46 shorter events, 8.6 us)
Async XLA Ops:
  1.7 9.9 %collective-permute-start = (f32[4,1,2048]{2,1,0:T(1,128)S(1)}, f32[4,1,2048]{2,1,0:T(1,128)S(1)}, u32[]{:S(2)}, u32[]{:S(2)}) collective-permute-start(f32[4,1,2048]{2,1,0:T(1,128)S(1)} %get-tuple-element.36), channel_id=1, source_target_pairs={{1,0},{2,1},{3,2},{5,4},{6,5},{7,6},{9,8},{10,9},{11,10},{13,12},{... | collective-permute-start | bytes 98312 | tf_op jit(solution)/shard_map/ppermute | solution.py:18
  3.0 8.6 %collective-permute-start.1 = (f32[4,1,2048]{2,1,0:T(1,128)S(1)}, f32[4,1,2048]{2,1,0:T(1,128)S(1)}, u32[]{:S(2)}, u32[]{:S(2)}) collective-permute-start(f32[4,1,2048]{2,1,0:T(1,128)S(1)} %get-tuple-element.37), channel_id=1, source_target_pairs={{0,1},{1,2},{2,3},{4,5},{5,6},{6,7},{8,9},{9,10},{10,11},{12,13},{... | collective-permute-start | bytes 98312 | tf_op jit(solution)/shard_map/ppermute | solution.py:17
  6.1 5.5 %copy-start = (f32[4,64,2048]{2,1,0:T(8,128)S(1)}, f32[4,64,2048]{2,1,0:T(8,128)}, u32[]{:S(2)}) copy-start(f32[4,64,2048]{2,1,0:T(8,128)} %param.4) | copy-start | bytes 6291460
  16.2 1.3 copy-start.4
  17.5 18.4 %collective-permute-start.2 = (f32[1,64,2048]{2,1,0:T(8,128)S(1)}, f32[1,64,2048]{2,1,0:T(8,128)S(1)}, u32[]{:S(2)}, u32[]{:S(2)}) collective-permute-start(f32[1,64,2048]{2,1,0:T(8,128)S(1)} %slice.172), channel_id=1, source_target_pairs={{0,4},{4,8},{8,12},{12,16},{16,20},{20,24},{24,28},{28,0},{1,5},{5... | collective-permute-start | bytes 1572872 | tf_op jit(solution)/shard_map/ppermute | solution.py:25
  36.4 14.2 %copy-start.3 = (f32[4,64,2048]{2,1,0:T(8,128)S(1)}, f32[4,64,2048]{2,1,0:T(8,128)}, u32[]{:S(2)}) copy-start(f32[4,64,2048]{2,1,0:T(8,128)} %param.5) | copy-start | bytes 6291460
  36.4 14.2 %collective-permute-start.3 = (f32[1,64,2048]{2,1,0:T(8,128)S(1)}, f32[1,64,2048]{2,1,0:T(8,128)S(1)}, u32[]{:S(2)}, u32[]{:S(2)}) collective-permute-start(f32[1,64,2048]{2,1,0:T(8,128)S(1)} %slice.175), channel_id=1, source_target_pairs={{0,28},{4,0},{8,4},{12,8},{16,12},{20,16},{24,20},{28,24},{1,29},{... | collective-permute-start | bytes 1572872 | tf_op jit(solution)/shard_map/ppermute | solution.py:25
  50.9 6.2 %copy-start.1 = (f32[4,64,2048]{2,1,0:T(8,128)}, f32[4,64,2048]{2,1,0:T(8,128)S(1)}, u32[]{:S(2)}) copy-start(f32[4,64,2048]{2,1,0:T(8,128)S(1)} %maximum_multiply_fusion.1) | copy-start | bytes 6291460
  51.0 6.1 %copy-start.5 = (f32[4,64,2048]{2,1,0:T(8,128)S(1)}, f32[4,64,2048]{2,1,0:T(8,128)}, u32[]{:S(2)}) copy-start(f32[4,64,2048]{2,1,0:T(8,128)} %param.3) | copy-start | bytes 6291460
  51.8 4.6 %collective-permute-start.4 = (f32[4,1,2048]{2,1,0:T(1,128)S(1)}, f32[4,1,2048]{2,1,0:T(1,128)S(1)}, u32[]{:S(2)}, u32[]{:S(2)}) collective-permute-start(f32[4,1,2048]{2,1,0:T(1,128)S(1)} %get-tuple-element.30), channel_id=1, source_target_pairs={{1,0},{2,1},{3,2},{5,4},{6,5},{7,6},{9,8},{10,9},{11,10},{13,12},{... | collective-permute-start | bytes 98312 | tf_op jit(solution)/shard_map/ppermute | solution.py:18
  53.2 3.9 %collective-permute-start.5 = (f32[4,1,2048]{2,1,0:T(1,128)S(1)}, f32[4,1,2048]{2,1,0:T(1,128)S(1)}, u32[]{:S(2)}, u32[]{:S(2)}) collective-permute-start(f32[4,1,2048]{2,1,0:T(1,128)S(1)} %get-tuple-element.31), channel_id=1, source_target_pairs={{0,1},{1,2},{2,3},{4,5},{5,6},{6,7},{8,9},{9,10},{10,11},{12,13},{... | collective-permute-start | bytes 98312 | tf_op jit(solution)/shard_map/ppermute | solution.py:17
  59.1 4.8 %collective-permute-start.6 = (f32[4,1,2048]{2,1,0:T(1,128)S(1)}, f32[4,1,2048]{2,1,0:T(1,128)S(1)}, u32[]{:S(2)}, u32[]{:S(2)}) collective-permute-start(f32[4,1,2048]{2,1,0:T(1,128)S(1)} %get-tuple-element.24), channel_id=1, source_target_pairs={{1,0},{2,1},{3,2},{5,4},{6,5},{7,6},{9,8},{10,9},{11,10},{13,12},{... | collective-permute-start | bytes 98312 | tf_op jit(solution)/shard_map/ppermute | solution.py:18
  60.4 4.2 %collective-permute-start.7 = (f32[4,1,2048]{2,1,0:T(1,128)S(1)}, f32[4,1,2048]{2,1,0:T(1,128)S(1)}, u32[]{:S(2)}, u32[]{:S(2)}) collective-permute-start(f32[4,1,2048]{2,1,0:T(1,128)S(1)} %get-tuple-element.25), channel_id=1, source_target_pairs={{0,1},{1,2},{2,3},{4,5},{5,6},{6,7},{8,9},{9,10},{10,11},{12,13},{... | collective-permute-start | bytes 98312 | tf_op jit(solution)/shard_map/ppermute | solution.py:17
  67.4 15.8 %collective-permute-start.8 = (f32[1,64,2048]{2,1,0:T(8,128)S(1)}, f32[1,64,2048]{2,1,0:T(8,128)S(1)}, u32[]{:S(2)}, u32[]{:S(2)}) collective-permute-start(f32[1,64,2048]{2,1,0:T(8,128)S(1)} %slice.188), channel_id=1, source_target_pairs={{0,4},{4,8},{8,12},{12,16},{16,20},{20,24},{24,28},{28,0},{1,5},{5... | collective-permute-start | bytes 1572872 | tf_op jit(solution)/shard_map/ppermute | solution.py:25
  83.6 14.2 %collective-permute-start.9 = (f32[1,64,2048]{2,1,0:T(8,128)S(1)}, f32[1,64,2048]{2,1,0:T(8,128)S(1)}, u32[]{:S(2)}, u32[]{:S(2)}) collective-permute-start(f32[1,64,2048]{2,1,0:T(8,128)S(1)} %slice.191), channel_id=1, source_target_pairs={{0,28},{4,0},{8,4},{12,8},{16,12},{20,16},{24,20},{28,24},{1,29},{... | collective-permute-start | bytes 1572872 | tf_op jit(solution)/shard_map/ppermute | solution.py:25
  98.3 6.0 %copy-start.2 = (f32[4,64,2048]{2,1,0:T(8,128)}, f32[4,64,2048]{2,1,0:T(8,128)S(1)}, u32[]{:S(2)}) copy-start(f32[4,64,2048]{2,1,0:T(8,128)S(1)} %maximum_multiply_fusion.3) | copy-start | bytes 6291460
  99.1 4.4 %collective-permute-start.10 = (f32[4,1,2048]{2,1,0:T(1,128)S(1)}, f32[4,1,2048]{2,1,0:T(1,128)S(1)}, u32[]{:S(2)}, u32[]{:S(2)}) collective-permute-start(f32[4,1,2048]{2,1,0:T(1,128)S(1)} %get-tuple-element.18), channel_id=1, source_target_pairs={{1,0},{2,1},{3,2},{5,4},{6,5},{7,6},{9,8},{10,9},{11,10},{13,12},{... | collective-permute-start | bytes 98312 | tf_op jit(solution)/shard_map/ppermute | solution.py:18
  100.4 3.9 %collective-permute-start.11 = (f32[4,1,2048]{2,1,0:T(1,128)S(1)}, f32[4,1,2048]{2,1,0:T(1,128)S(1)}, u32[]{:S(2)}, u32[]{:S(2)}) collective-permute-start(f32[4,1,2048]{2,1,0:T(1,128)S(1)} %get-tuple-element.19), channel_id=1, source_target_pairs={{0,1},{1,2},{2,3},{4,5},{5,6},{6,7},{8,9},{9,10},{10,11},{12,13},{... | collective-permute-start | bytes 98312 | tf_op jit(solution)/shard_map/ppermute | solution.py:17
where the time goes:
time: 163 us; the launch traced here: 162 us
  waiting for transfers between devices  55.2 us (34%)
  blocking collectives  43.2 us (27%)
  starting transfers between devices  25.5 us (16%)
  other arithmetic  23.6 us (14%)
  local copies, waits for them, and re-layouts  12.3 us (8%)
  between operations  2.31 us (1%)
    ppermute x4, waiting for transfers between devices, from_behind(): return lax.ppermute(x, axis, [(i, (i + by) % count) for i in range(count)])  53 us
    psum x1, blocking collectives, on_device(): norm_sq = lax.psum(jnp.sum(residual * residual), ('tm', 'slab'))  43.2 us
    ppermute x4, starting transfers between devices, padded_2(): before = lax.ppermute(last, axis, up)  12.4 us
    sub x1, other arithmetic, on_device(): residual_new = residual - alpha * applied  9.78 us
    slice x8, local copies, waits for them, and re-layouts, hopping(): sideways = jnp.roll(center, 1, axis=2) + jnp.roll(center, -1, axis=2)  7.75 us
    ppermute x4, starting transfers between devices, from_behind(): return lax.ppermute(x, axis, [(i, (i + by) % count) for i in range(count)])  7.73 us
    mul x2, other arithmetic, forward(): carried = weights * hopped  7.24 us
    ppermute x4, starting transfers between devices, padded_2(): after = lax.ppermute(leading, axis, down)  5.3 us
  transfers between devices with their start and end apart: 12, of which 7 were waited for; matrix products, arithmetic and copies ran while one was open for 5% of the time, Pallas kernels for 0%

commit v1 on v0

v1 whole, which is shorter than its diff:
```python
import functools

import jax
import jax.numpy as jnp
from jax import lax
from jax.experimental import pallas as pl
from jax.experimental.pallas import tpu as pltpu
from jax.sharding import PartitionSpec as P

HOP_WEIGHT = 0.125
BOSON_WEIGHT = 2.0
MESH = pl.DeviceIdType.MESH
TILE = 8
LANES = 128


def kernel(
    nt, ns, L, R, C,
    src_h, g_h, f_h, sol_o, rn_o, fo_o,
    gp, bp, rp, qp, f, q, hg, hr, im, w, car, carr, c0, gN, cin, cN, rin,
    acc, slabg, tmg,
    lsem, osem, hss, hrs, bss, brs, css, crs, s1s, s1r, s2s, s2r,
):
    NB = R // TILE
    last = L - 1
    tm, sl = lax.axis_index("tm"), lax.axis_index("slab")
    nxt_t, prv_t = lax.rem(tm + 1, nt), lax.rem(tm + nt - 1, nt)
    up_s, dn_s = lax.rem(sl + ns - 1, ns), lax.rem(sl + 1, ns)
    has_up, has_dn = sl > 0, sl < ns - 1
    s_b = jnp.where(tm == 0, -1.0, 1.0).astype(jnp.float32)
    s_n = jnp.where(tm == nt - 1, -1.0, 1.0).astype(jnp.float32)

    order = [last] + list(range(last))
    g_in = {t: pltpu.make_async_copy(g_h.at[t], gp.at[t, pl.ds(TILE, R)], lsem.at[0, t]) for t in order}
    f_in = {t: pltpu.make_async_copy(f_h.at[t], f.at[t], lsem.at[1, t]) for t in order}
    q_in = {t: pltpu.make_async_copy(src_h.at[t], q.at[t], lsem.at[2, t]) for t in order}
    for t in order:
        g_in[t].start()
        f_in[t].start()
    for t in range(L):
        q_in[t].start()

    barrier = pltpu.get_barrier_semaphore()
    for k in range(1, ns):
        pl.semaphore_signal(barrier, inc=1, device_id=(tm, lax.rem(sl + k, ns)), device_id_type=MESH)
    for k in range(1, nt):
        pl.semaphore_signal(barrier, inc=1, device_id=(lax.rem(tm + k, nt), sl), device_id_type=MESH)
    pl.semaphore_wait(barrier, ns - 1 + nt - 1)

    def to_prev(src, dst, k):
        return pltpu.make_async_remote_copy(
            src_ref=src, dst_ref=dst, send_sem=bss.at[k], recv_sem=brs.at[k],
            device_id=(prv_t, sl), device_id_type=MESH)

    def to_next(src, dst, send, recv):
        return pltpu.make_async_remote_copy(
            src_ref=src, dst_ref=dst, send_sem=send, recv_sem=recv,
            device_id=(nxt_t, sl), device_id_type=MESH)

    def halo(src, off, dst, lo, n, k):
        ts = pl.ds(lo, n)
        up = pltpu.make_async_remote_copy(
            src_ref=src.at[ts, pl.ds(off, TILE)], dst_ref=dst.at[ts, pl.ds(TILE + R, TILE)],
            send_sem=hss.at[k, 0], recv_sem=hrs.at[k, 0],
            device_id=(tm, up_s), device_id_type=MESH)
        dn = pltpu.make_async_remote_copy(
            src_ref=src.at[ts, pl.ds(off + R - TILE, TILE)], dst_ref=dst.at[ts, pl.ds(0, TILE)],
            send_sem=hss.at[k, 1], recv_sem=hrs.at[k, 1],
            device_id=(tm, dn_s), device_id_type=MESH)

        @pl.when(has_up)
        def _():
            up.start()

        @pl.when(has_dn)
        def _():
            dn.start()

        def wait():
            @pl.when(has_up)
            def _():
                up.wait_send()
                dn.wait_recv()

            @pl.when(has_dn)
            def _():
                dn.wait_send()
                up.wait_recv()

        return wait

    send_g = to_prev(g_h.at[0], gN, 0)
    send_g.start()
    x1 = halo(g_h, 0, gp, 0, L, 0)

    @pl.when(jnp.logical_not(has_up))
    def _():
        for p in (gp, bp, rp, qp):
            for t in range(L):
                p[t, 0:TILE, :] = jnp.zeros((TILE, C), jnp.float32)

    @pl.when(jnp.logical_not(has_dn))
    def _():
        for p in (gp, bp, rp, qp):
            for t in range(L):
                p[t, TILE + R:, :] = jnp.zeros((TILE, C), jnp.float32)

    sub = lax.broadcasted_iota(jnp.int32, (TILE, C), 0)
    col = lax.broadcasted_iota(jnp.int32, (TILE, C), 1)
    even = lax.rem(sub + col, 2) == 0

    def rows(i, pad=0):
        return pl.ds(pl.multiple_of(i * TILE + pad, TILE), TILE)

    def hop(p, t, i):
        cur = p[t, rows(i, TILE), :]
        below = pltpu.roll(jnp.where(sub == 0, p[t, rows(i, 2 * TILE), :], cur), TILE - 1, 0)
        above = pltpu.roll(jnp.where(sub == TILE - 1, p[t, rows(i), :], cur), 1, 0)
        side = pltpu.roll(cur, 1, 1) + pltpu.roll(cur, C - 1, 1)
        return cur, cur + HOP_WEIGHT * (side + jnp.where(even, below, above))

    def fold(x):
        x = x * x
        parts = [x[:, k * LANES:(k + 1) * LANES] for k in range(C // LANES)]
        while len(parts) > 1:
            odd = parts[len(parts) // 2 * 2:]
            parts = [a + b for a, b in zip(parts[::2], parts[1::2])] + odd
        return parts[0]

    def each(n, body, init=0):
        return lax.fori_loop(0, n * NB, lambda j, c: body(j // NB, j % NB, c), init)

    for t in order:
        g_in[t].wait()
        f_in[t].wait()
    x1()

    def body_a(_, i, c):
        cur, k = hop(gp, last, i)
        wv = jnp.exp(f[last, rows(i), :])
        w[last, rows(i), :] = wv
        hg[last, rows(i), :] = k
        car[rows(i), :] = wv * k
        return c

    each(1, body_a)
    send_car = to_next(car, cin, bss.at[1], brs.at[1])
    send_car.start()

    for t in range(L):
        q_in[t].wait()

    def body_b0(_, i, c):
        q[0, rows(i), :] = q[0, rows(i), :] - gp[0, rows(i, TILE), :]
        return c

    each(1, body_b0)

    def body_b(t, i, c):
        cur, k = hop(gp, t, i)
        wv = jnp.exp(f[t, rows(i), :])
        w[t, rows(i), :] = wv
        hg[t, rows(i), :] = k
        image = gp[t + 1, rows(i, TILE), :] - wv * k
        q[t + 1, rows(i), :] = q[t + 1, rows(i), :] - image
        bp[t, rows(i, TILE), :] = wv * image
        return c

    each(last, body_b)
    x2a = halo(bp, TILE, bp, 0, last, 1)
    x2a()

    def body_c(_, i, c):
        cur, k = hop(bp, 0, i)
        c0[rows(i), :] = q[0, rows(i), :] + k
        return c

    each(1, body_c)
    send_c = to_prev(c0, cN, 2)
    send_c.start()

    zero = jnp.zeros((TILE, LANES), jnp.float32)

    def body_r(base):
        def body(t, i, c):
            t = t + base
            cur, k = hop(bp, t, i)
            r = q[t, rows(i), :] + k
            rp[t, rows(i, TILE), :] = r
            return c + fold(r)
        return body

    norm = each(last - 1, body_r(1), zero)

    send_g.wait_recv()

    def body_d(_, i, c):
        image = s_n * gN[rows(i), :] - car[rows(i), :]
        bp[last, rows(i, TILE), :] = w[last, rows(i), :] * image
        return c

    each(1, body_d)
    x2b = halo(bp, TILE, bp, last, 1, 2)
    x2b()
    norm = each(1, body_r(last), norm)
    x3a = halo(rp, TILE, rp, 1, last, 3)
    x3a()

    def body_e(_, i, c):
        cur, k = hop(rp, last, i)
        hr[last, rows(i), :] = k
        carr[rows(i), :] = w[last, rows(i), :] * k
        return c

    each(1, body_e)
    send_r = [to_next(carr.at[pl.ds(i * TILE, TILE)], rin.at[pl.ds(i * TILE, TILE)], css.at[i], crs.at[i])
              for i in range(NB)]
    early = NB // 2
    for i in range(early):
        send_r[i].start()

    def body_f(base):
        def body(t, i, c):
            t = t + base
            cur, k = hop(rp, t, i)
            hr[t, rows(i), :] = k
            wv = w[t, rows(i), :]
            image = rp[t + 1, rows(i, TILE), :] - wv * k
            im[t + 1, rows(i), :] = image
            qp[t, rows(i, TILE), :] = wv * image
            return c + fold(image)
        return body

    curv = each(last - 1, body_f(1), zero)

    send_car.wait_recv()

    def body_g(_, i, c):
        r = c0[rows(i), :] + s_b * cin[rows(i), :]
        rp[0, rows(i, TILE), :] = r
        return c + fold(r)

    norm = each(1, body_g, norm)
    x3b = halo(rp, TILE, rp, 0, 1, 4)
    x3b()
    curv = each(1, body_f(0), curv)
    x4a = halo(qp, TILE, qp, 0, last, 5)
    x4a()

    def body_y(base):
        def body(t, i, c):
            t = t + base
            cur, k = hop(qp, t, i)
            im[t, rows(i), :] = im[t, rows(i), :] - k
            return c
        return body

    def body_y0(_, i, c):
        cur, k = hop(qp, 0, i)
        im[0, rows(i), :] = rp[0, rows(i, TILE), :] - k
        return c

    each(1, body_y0)
    each(last - 1, body_y(1))

    send_c.wait_recv()

    def body_h(_, i, c):
        carried = carr[rows(i), :]
        r_next = cN[rows(i), :] + s_n * car[rows(i), :]
        image = s_n * r_next - carried
        qp[last, rows(i, TILE), :] = w[last, rows(i), :] * image
        return c + fold(image)

    curv = each(1, body_h, curv)
    acc[0, 0] = norm
    acc[0, 1] = curv
    slabg[sl, 0] = norm
    slabg[sl, 1] = curv
    sum1 = []
    for k in range(1, ns):
        sum1.append(pltpu.make_async_remote_copy(
            src_ref=acc.at[0], dst_ref=slabg.at[sl], send_sem=s1s.at[k], recv_sem=s1r.at[k],
            device_id=(tm, lax.rem(sl + k, ns)), device_id_type=MESH))
        sum1[-1].start()
    x4b = halo(qp, TILE, qp, last, 1, 6)
    for k in range(1, ns):
        pltpu.make_async_remote_copy(
            src_ref=acc.at[0], dst_ref=slabg.at[lax.rem(sl + ns - k, ns)], send_sem=s1s.at[k], recv_sem=s1r.at[k],
            device_id=(tm, lax.rem(sl + k, ns)), device_id_type=MESH).wait_recv()
    total = slabg[0]
    for k in range(1, ns):
        total = total + slabg[k]
    acc[1] = total
    tmg[tm] = total
    sum2 = []
    for k in range(1, nt):
        sum2.append(pltpu.make_async_remote_copy(
            src_ref=acc.at[1], dst_ref=tmg.at[tm], send_sem=s2s.at[k], recv_sem=s2r.at[k],
            device_id=(lax.rem(tm + k, nt), sl), device_id_type=MESH))
        sum2[-1].start()
    for i in range(early, NB):
        send_r[i].start()
    x4b()
    each(1, body_y(last))
    for k in range(1, nt):
        pltpu.make_async_remote_copy(
            src_ref=acc.at[1], dst_ref=tmg.at[lax.rem(tm + nt - k, nt)], send_sem=s2s.at[k], recv_sem=s2r.at[k],
            device_id=(lax.rem(tm + k, nt), sl), device_id_type=MESH).wait_recv()
    total = tmg[0]
    for k in range(1, nt):
        total = total + tmg[k]
    alpha = (jnp.full((TILE, C), jnp.sum(total[0])) / jnp.full((TILE, C), jnp.sum(total[1])))

    def body_s(t, i, c):
        r = rp[t, rows(i, TILE), :]
        gp[t, rows(i, TILE), :] = gp[t, rows(i, TILE), :] + alpha * r
        back = bp[t, rows(i, TILE), :] + alpha * qp[t, rows(i, TILE), :]
        hopped = hg[t, rows(i), :] + alpha * hr[t, rows(i), :]
        f[t, rows(i), :] = BOSON_WEIGHT * f[t, rows(i), :] + 2.0 * (back * hopped)
        return c

    each(L, body_s)
    outs = []
    for t in range(L):
        outs.append(pltpu.make_async_copy(gp.at[t, pl.ds(TILE, R)], sol_o.at[t], osem.at[0, t]))
        outs.append(pltpu.make_async_copy(f.at[t], fo_o.at[t], osem.at[1, t]))
    for o in outs:
        o.start()

    def body_n(t, i, c):
        t = t + 1
        q[t, rows(i), :] = rp[t, rows(i, TILE), :] - alpha * im[t, rows(i), :]
        return c

    each(last, body_n)
    for t in range(1, L):
        outs.append(pltpu.make_async_copy(q.at[t], rn_o.at[t], osem.at[2, t]))
        outs[-1].start()
    for i in range(NB):
        send_r[i].wait_recv()
        d = pl.ds(i * TILE, TILE)
        q[0, d, :] = rp[0, pl.ds(TILE + i * TILE, TILE), :] - alpha * (im[0, d, :] - s_b * rin[d, :])
    outs.append(pltpu.make_async_copy(q.at[0], rn_o.at[0], osem.at[2, 0]))
    outs[-1].start()
    send_g.wait_send()
    send_car.wait_send()
    send_c.wait_send()
    for c in send_r + sum1 + sum2:
        c.wait_send()
    for o in outs:
        o.wait()


def on_device(source, guess, field):
    L, R, C = source.shape
    nt, ns = lax.axis_size("tm"), lax.axis_size("slab")
    NB = R // TILE
    f32 = jnp.float32
    padded = pltpu.VMEM((L, R + 2 * TILE, C), f32)
    whole = pltpu.VMEM((L, R, C), f32)
    one = pltpu.VMEM((R, C), f32)
    sems = lambda *shape: pltpu.SemaphoreType.DMA(shape)
    return pl.pallas_call(
        functools.partial(kernel, nt, ns, L, R, C),
        out_shape=[jax.ShapeDtypeStruct((L, R, C), f32)] * 3,
        in_specs=[pl.BlockSpec(memory_space=pl.ANY)] * 3,
        out_specs=[pl.BlockSpec(memory_space=pl.ANY)] * 3,
        scratch_shapes=[padded] * 4 + [whole] * 6 + [one] * 7 + [
            pltpu.VMEM((2, 2, TILE, LANES), f32),
            pltpu.VMEM((ns, 2, TILE, LANES), f32),
            pltpu.VMEM((nt, 2, TILE, LANES), f32),
            sems(3, L), sems(3, L), sems(7, 2), sems(7, 2), sems(3), sems(3),
            sems(NB), sems(NB), sems(ns), sems(ns), sems(nt), sems(nt),
        ],
        compiler_params=pltpu.CompilerParams(
            collective_id=0, has_side_effects=True, vmem_limit_bytes=48 * 1024 * 1024),
    )(source, guess, field)


def solution(mesh):
    specs = (P("tm", "slab", None),) * 3
    return jax.shard_map(on_device, mesh=mesh, in_specs=specs, out_specs=specs, check_vma=False)
```

time: 163 us -> 74.2 us (0.46)
  Pallas kernels: 0 us -> 68.4 us
  waiting for transfers between devices: 55.2 us -> 0 us
  blocking collectives: 43.2 us -> 0 us
  starting transfers between devices: 25.5 us -> 0 us
  other arithmetic: 23.6 us -> 0 us
  local copies, waits for them, and re-layouts: 12.3 us -> 4.99 us
  between operations: 2.31 us -> 0.64 us
    pallas_call x0 -> x1, Pallas kernels: none -> 68.4 us  [on_device(): pl.pallas_call(functools.partial(kernel, nt, ns, L, R, C), out_shape=[jax...]
    ppermute x12 -> x0, waiting for transfers between devices: 55.2 us -> none  [the longest x4 53 us: from_behind(): return lax.ppermute(x, axis, [(i, (i + by) % count) for i in range(count)])]
    psum x1 -> x0, blocking collectives: 43.2 us -> none  [on_device(): norm_sq = lax.psum(jnp.sum(residual * residual), ('tm', 'slab'))]
    ppermute x12 -> x0, starting transfers between devices: 25.5 us -> none  [the longest x4 12.4 us: padded_2(): before = lax.ppermute(last, axis, up)]
    sub x4 -> x0, other arithmetic: 11.8 us -> none  [the longest x1 9.78 us: on_device(): residual_new = residual - alpha * applied]
    slice x20 -> x0, local copies, waits for them, and re-layouts: 10.9 us -> none  [the longest x8 7.75 us: hopping(): sideways = jnp.roll(center, 1, axis=2) + jnp.roll(center, -1, axis=2)]
    mul x4 -> x0, other arithmetic: 7.96 us -> none  [the longest x2 7.24 us: forward(): carried = weights * hopped]
    unnamed x12 -> x5, local copies, waits for them, and re-layouts: 1.35 us -> 4.99 us
  transfers between devices with their start and end apart: 12 -> 0, of which waited for: 7 -> 0; matrix products, arithmetic and copies ran while one was open for 5% -> 0% of each run, Pallas kernels for 0% -> 0%
where the time goes in v1:
time: 74.2 us; the launch traced here: 74 us
  Pallas kernels  68.4 us (92%)
  local copies, waits for them, and re-layouts  4.99 us (7%)
    pallas_call x1, Pallas kernels, on_device(): pl.pallas_call(functools.partial(kernel, nt, ns, L, R, C), out_shape=[jax...  68.4 us
    unnamed x5, local copies, waits for them, and re-layouts  4.99 us

profile of v1, /device:TPU:0, one launch (start us, length us, event | category | flops | bytes accessed | tf_op | source)
XLA Modules:
  0.0 74.0 jit_solution(9320339658640094130)
XLA Ops:
  0.6 68.4 %shard_map.58 = (f32[4,64,2048]{2,1,0:T(8,128)S(1)}, f32[4,64,2048]{2,1,0:T(8,128)S(1)}, f32[4,64,2048]{2,1,0:T(8,128)}) custom-call(f32[4,64,2048]{2,1,0:T(8,128)} %src_h.1, f32[4,64,2048]{2,1,0:T(8,128)} %g_h.1, f32[4,64,2048]{2,1,0:T(8,128)} %f_h.1), custom_call_target="tpu_custom_call" | custom-call | tf_op jit(solution)/shard_map/pallas_call | solution.py:364
  69.0 1.3 %copy.9 = f32[4,64,2048]{2,1,0:T(8,128)} copy(f32[4,64,2048]{2,1,0:T(8,128)S(1)} %get-tuple-element.6) | data formatting | bytes 4194304
  70.3 0.0 copy-start
  70.3 1.3 %copy.10 = f32[4,64,2048]{2,1,0:T(8,128)} copy(f32[4,64,2048]{2,1,0:T(8,128)S(1)} %get-tuple-element.7) | data formatting | bytes 4194304
  71.7 1.0 %copy-done = f32[4,64,2048]{2,1,0:T(8,128)S(1)} copy-done((f32[4,64,2048]{2,1,0:T(8,128)S(1)}, f32[4,64,2048]{2,1,0:T(8,128)}, u32[]{:S(2)}) %copy-start) | copy-done | bytes 2097176
  72.7 1.3 %copy.11 = f32[4,64,2048]{2,1,0:T(8,128)} copy(f32[4,64,2048]{2,1,0:T(8,128)S(1)} %copy-done) | data formatting | bytes 4194304
Async XLA Ops:
  70.3 2.3 %copy-start = (f32[4,64,2048]{2,1,0:T(8,128)S(1)}, f32[4,64,2048]{2,1,0:T(8,128)}, u32[]{:S(2)}) copy-start(f32[4,64,2048]{2,1,0:T(8,128)} %get-tuple-element.8) | copy-start | bytes 6291460

commit v2 on v1

--- a/solution.py
+++ b/solution.py
@@ -19,7 +19,7 @@
     src_h, g_h, f_h, sol_o, rn_o, fo_o,
     gp, bp, rp, qp, f, q, hg, hr, im, w, car, carr, c0, gN, cin, cN, rin,
     acc, slabg, tmg,
-    lsem, osem, hss, hrs, bss, brs, css, crs, s1s, s1r, s2s, s2r,
+    lsem, hss, hrs, bss, brs, css, crs, s1s, s1r, s2s, s2r,
 ):
     NB = R // TILE
     last = L - 1
@@ -60,11 +60,11 @@
     def halo(src, off, dst, lo, n, k):
         ts = pl.ds(lo, n)
         up = pltpu.make_async_remote_copy(
-            src_ref=src.at[ts, pl.ds(off, TILE)], dst_ref=dst.at[ts, pl.ds(TILE + R, TILE)],
+            src_ref=src.at[ts, pl.ds(off, 1)], dst_ref=dst.at[ts, pl.ds(TILE + R, 1)],
             send_sem=hss.at[k, 0], recv_sem=hrs.at[k, 0],
             device_id=(tm, up_s), device_id_type=MESH)
         dn = pltpu.make_async_remote_copy(
-            src_ref=src.at[ts, pl.ds(off + R - TILE, TILE)], dst_ref=dst.at[ts, pl.ds(0, TILE)],
+            src_ref=src.at[ts, pl.ds(off + R - 1, 1)], dst_ref=dst.at[ts, pl.ds(TILE - 1, 1)],
             send_sem=hss.at[k, 1], recv_sem=hrs.at[k, 1],
             device_id=(tm, dn_s), device_id_type=MESH)
 
@@ -106,8 +106,9 @@
                 p[t, TILE + R:, :] = jnp.zeros((TILE, C), jnp.float32)
 
     sub = lax.broadcasted_iota(jnp.int32, (TILE, C), 0)
-    col = lax.broadcasted_iota(jnp.int32, (TILE, C), 1)
-    even = lax.rem(sub + col, 2) == 0
+    parity = lax.rem(
+        lax.broadcasted_iota(jnp.int32, (TILE, LANES), 0) + lax.broadcasted_iota(jnp.int32, (TILE, LANES), 1), 2)
+    even = jnp.concatenate([parity] * (C // LANES), axis=1) == 0
 
     def rows(i, pad=0):
         return pl.ds(pl.multiple_of(i * TILE + pad, TILE), TILE)
@@ -130,9 +131,10 @@
     def each(n, body, init=0):
         return lax.fori_loop(0, n * NB, lambda j, c: body(j // NB, j % NB, c), init)
 
-    for t in order:
-        g_in[t].wait()
-        f_in[t].wait()
+    zero = jnp.zeros((TILE, LANES), jnp.float32)
+
+    g_in[last].wait()
+    f_in[last].wait()
     x1()
 
     def body_a(_, i, c):
@@ -147,39 +149,39 @@
     send_car = to_next(car, cin, bss.at[1], brs.at[1])
     send_car.start()
 
+    for t in range(last):
+        g_in[t].wait()
+        f_in[t].wait()
     for t in range(L):
         q_in[t].wait()
 
-    def body_b0(_, i, c):
-        q[0, rows(i), :] = q[0, rows(i), :] - gp[0, rows(i, TILE), :]
-        return c
-
-    each(1, body_b0)
-
-    def body_b(t, i, c):
-        cur, k = hop(gp, t, i)
-        wv = jnp.exp(f[t, rows(i), :])
-        w[t, rows(i), :] = wv
-        hg[t, rows(i), :] = k
-        image = gp[t + 1, rows(i, TILE), :] - wv * k
-        q[t + 1, rows(i), :] = q[t + 1, rows(i), :] - image
-        bp[t, rows(i, TILE), :] = wv * image
-        return c
-
-    each(last, body_b)
-    x2a = halo(bp, TILE, bp, 0, last, 1)
-    x2a()
+    def body_b(base):
+        def body(t, i, c):
+            t = t + base
+            cur, k = hop(gp, t, i)
+            wv = jnp.exp(f[t, rows(i), :])
+            w[t, rows(i), :] = wv
+            hg[t, rows(i), :] = k
+            image = gp[t + 1, rows(i, TILE), :] - wv * k
+            q[t + 1, rows(i), :] = q[t + 1, rows(i), :] - image
+            bp[t, rows(i, TILE), :] = wv * image
+            return c
+        return body
+
+    each(1, body_b(0))
+    x2c = halo(bp, TILE, bp, 0, 1, 7)
+    each(last - 1, body_b(1))
+    x2a = halo(bp, TILE, bp, 1, last - 1, 1)
+    x2c()
 
     def body_c(_, i, c):
         cur, k = hop(bp, 0, i)
-        c0[rows(i), :] = q[0, rows(i), :] + k
+        c0[rows(i), :] = (q[0, rows(i), :] - gp[0, rows(i, TILE), :]) + k
         return c
 
     each(1, body_c)
     send_c = to_prev(c0, cN, 2)
     send_c.start()
-
-    zero = jnp.zeros((TILE, LANES), jnp.float32)
 
     def body_r(base):
         def body(t, i, c):
@@ -190,8 +192,7 @@
             return c + fold(r)
         return body
 
-    norm = each(last - 1, body_r(1), zero)
-
+    x2a()
     send_g.wait_recv()
 
     def body_d(_, i, c):
@@ -201,9 +202,12 @@
 
     each(1, body_d)
     x2b = halo(bp, TILE, bp, last, 1, 2)
+    norm = each(last - 1, body_r(1), zero)
+    x3c = halo(rp, TILE, rp, 1, last - 1, 8)
     x2b()
     norm = each(1, body_r(last), norm)
-    x3a = halo(rp, TILE, rp, 1, last, 3)
+    x3a = halo(rp, TILE, rp, last, 1, 3)
+    x3c()
     x3a()
 
     def body_e(_, i, c):
@@ -215,7 +219,7 @@
     each(1, body_e)
     send_r = [to_next(carr.at[pl.ds(i * TILE, TILE)], rin.at[pl.ds(i * TILE, TILE)], css.at[i], crs.at[i])
               for i in range(NB)]
-    early = NB // 2
+    early = NB * 5 // 8
     for i in range(early):
         send_r[i].start()
 
@@ -231,8 +235,6 @@
             return c + fold(image)
         return body
 
-    curv = each(last - 1, body_f(1), zero)
-
     send_car.wait_recv()
 
     def body_g(_, i, c):
@@ -242,10 +244,10 @@
 
     norm = each(1, body_g, norm)
     x3b = halo(rp, TILE, rp, 0, 1, 4)
+    curv = each(last - 1, body_f(1), zero)
     x3b()
     curv = each(1, body_f(0), curv)
     x4a = halo(qp, TILE, qp, 0, last, 5)
-    x4a()
 
     def body_y(base):
         def body(t, i, c):
@@ -260,9 +262,6 @@
         im[0, rows(i), :] = rp[0, rows(i, TILE), :] - k
         return c
 
-    each(1, body_y0)
-    each(last - 1, body_y(1))
-
     send_c.wait_recv()
 
     def body_h(_, i, c):
@@ -277,79 +276,76 @@
     acc[0, 1] = curv
     slabg[sl, 0] = norm
     slabg[sl, 1] = curv
-    sum1 = []
-    for k in range(1, ns):
-        sum1.append(pltpu.make_async_remote_copy(
-            src_ref=acc.at[0], dst_ref=slabg.at[sl], send_sem=s1s.at[k], recv_sem=s1r.at[k],
-            device_id=(tm, lax.rem(sl + k, ns)), device_id_type=MESH))
-        sum1[-1].start()
+
+    def gather(at, dst, axis, me, n, send, recv):
+        def copy(k, slot):
+            other = lax.rem(me + k, n)
+            return pltpu.make_async_remote_copy(
+                src_ref=acc.at[at], dst_ref=dst.at[slot], send_sem=send.at[k], recv_sem=recv.at[k],
+                device_id=(other, sl) if axis == 0 else (tm, other), device_id_type=MESH)
+        sent = [copy(k, me) for k in range(1, n)]
+        for c in sent:
+            c.start()
+
+        def wait():
+            for k in range(1, n):
+                copy(k, lax.rem(me + n - k, n)).wait_recv()
+            total = dst[0]
+            for k in range(1, n):
+                total = total + dst[k]
+            return total
+        return sent, wait
+
+    sum1, wait1 = gather(0, slabg, 1, sl, ns, s1s, s1r)
     x4b = halo(qp, TILE, qp, last, 1, 6)
-    for k in range(1, ns):
-        pltpu.make_async_remote_copy(
-            src_ref=acc.at[0], dst_ref=slabg.at[lax.rem(sl + ns - k, ns)], send_sem=s1s.at[k], recv_sem=s1r.at[k],
-            device_id=(tm, lax.rem(sl + k, ns)), device_id_type=MESH).wait_recv()
-    total = slabg[0]
-    for k in range(1, ns):
-        total = total + slabg[k]
+    total = wait1()
     acc[1] = total
     tmg[tm] = total
-    sum2 = []
-    for k in range(1, nt):
-        sum2.append(pltpu.make_async_remote_copy(
-            src_ref=acc.at[1], dst_ref=tmg.at[tm], send_sem=s2s.at[k], recv_sem=s2r.at[k],
-            device_id=(lax.rem(tm + k, nt), sl), device_id_type=MESH))
-        sum2[-1].start()
+    sum2, wait2 = gather(1, tmg, 0, tm, nt, s2s, s2r)
     for i in range(early, NB):
         send_r[i].start()
+    x4a()
+    each(1, body_y0)
+    each(last - 1, body_y(1))
     x4b()
     each(1, body_y(last))
-    for k in range(1, nt):
-        pltpu.make_async_remote_copy(
-            src_ref=acc.at[1], dst_ref=tmg.at[lax.rem(tm + nt - k, nt)], send_sem=s2s.at[k], recv_sem=s2r.at[k],
-            device_id=(lax.rem(tm + k, nt), sl), device_id_type=MESH).wait_recv()
-    total = tmg[0]
-    for k in range(1, nt):
-        total = total + tmg[k]
-    alpha = (jnp.full((TILE, C), jnp.sum(total[0])) / jnp.full((TILE, C), jnp.sum(total[1])))
+    total = wait2()
+    ratio = jnp.full((TILE, LANES), jnp.sum(total[0])) / jnp.full((TILE, LANES), jnp.sum(total[1]))
+    alpha = jnp.concatenate([ratio] * (C // LANES), axis=1)
 
     def body_s(t, i, c):
-        r = rp[t, rows(i, TILE), :]
-        gp[t, rows(i, TILE), :] = gp[t, rows(i, TILE), :] + alpha * r
+        sol_o[t, rows(i), :] = gp[t, rows(i, TILE), :] + alpha * rp[t, rows(i, TILE), :]
         back = bp[t, rows(i, TILE), :] + alpha * qp[t, rows(i, TILE), :]
         hopped = hg[t, rows(i), :] + alpha * hr[t, rows(i), :]
-        f[t, rows(i), :] = BOSON_WEIGHT * f[t, rows(i), :] + 2.0 * (back * hopped)
+        fo_o[t, rows(i), :] = BOSON_WEIGHT * f[t, rows(i), :] + 2.0 * (back * hopped)
         return c
 
     each(L, body_s)
-    outs = []
-    for t in range(L):
-        outs.append(pltpu.make_async_copy(gp.at[t, pl.ds(TILE, R)], sol_o.at[t], osem.at[0, t]))
-        outs.append(pltpu.make_async_copy(f.at[t], fo_o.at[t], osem.at[1, t]))
-    for o in outs:
-        o.start()
 
     def body_n(t, i, c):
         t = t + 1
-        q[t, rows(i), :] = rp[t, rows(i, TILE), :] - alpha * im[t, rows(i), :]
+        rn_o[t, rows(i), :] = rp[t, rows(i, TILE), :] - alpha * im[t, rows(i), :]
         return c
 
     each(last, body_n)
-    for t in range(1, L):
-        outs.append(pltpu.make_async_copy(q.at[t], rn_o.at[t], osem.at[2, t]))
-        outs[-1].start()
     for i in range(NB):
         send_r[i].wait_recv()
         d = pl.ds(i * TILE, TILE)
-        q[0, d, :] = rp[0, pl.ds(TILE + i * TILE, TILE), :] - alpha * (im[0, d, :] - s_b * rin[d, :])
-    outs.append(pltpu.make_async_copy(q.at[0], rn_o.at[0], osem.at[2, 0]))
-    outs[-1].start()
+        rn_o[0, d, :] = rp[0, pl.ds(TILE + i * TILE, TILE), :] - alpha * (im[0, d, :] - s_b * rin[d, :])
     send_g.wait_send()
     send_car.wait_send()
     send_c.wait_send()
     for c in send_r + sum1 + sum2:
         c.wait_send()
-    for o in outs:
-        o.wait()
+
+
+def write_out(L, a, b, c, x, y, z, sem):
+    copies = [pltpu.make_async_copy(src.at[t], dst.at[t], sem.at[j, t])
+              for j, (src, dst) in enumerate(((a, x), (b, y), (c, z))) for t in range(L)]
+    for copy in copies:
+        copy.start()
+    for copy in copies:
+        copy.wait()
 
 
 def on_device(source, guess, field):
@@ -361,21 +357,29 @@
     whole = pltpu.VMEM((L, R, C), f32)
     one = pltpu.VMEM((R, C), f32)
     sems = lambda *shape: pltpu.SemaphoreType.DMA(shape)
-    return pl.pallas_call(
+    outs = pl.pallas_call(
         functools.partial(kernel, nt, ns, L, R, C),
         out_shape=[jax.ShapeDtypeStruct((L, R, C), f32)] * 3,
-        in_specs=[pl.BlockSpec(memory_space=pl.ANY)] * 3,
-        out_specs=[pl.BlockSpec(memory_space=pl.ANY)] * 3,
+        in_specs=[pl.BlockSpec(memory_space=pltpu.HBM)] * 3,
+        out_specs=[pl.BlockSpec(memory_space=pltpu.VMEM)] * 3,
         scratch_shapes=[padded] * 4 + [whole] * 6 + [one] * 7 + [
             pltpu.VMEM((2, 2, TILE, LANES), f32),
             pltpu.VMEM((ns, 2, TILE, LANES), f32),
             pltpu.VMEM((nt, 2, TILE, LANES), f32),
-            sems(3, L), sems(3, L), sems(7, 2), sems(7, 2), sems(3), sems(3),
+            sems(3, L), sems(9, 2), sems(9, 2), sems(3), sems(3),
             sems(NB), sems(NB), sems(ns), sems(ns), sems(nt), sems(nt),
         ],
         compiler_params=pltpu.CompilerParams(
-            collective_id=0, has_side_effects=True, vmem_limit_bytes=48 * 1024 * 1024),
+            collective_id=0, has_side_effects=True, vmem_limit_bytes=57 * 1024 * 1024),
     )(source, guess, field)
+    return pl.pallas_call(
+        functools.partial(write_out, L),
+        out_shape=[jax.ShapeDtypeStruct((L, R, C), f32)] * 3,
+        in_specs=[pl.BlockSpec(memory_space=pltpu.VMEM)] * 3,
+        out_specs=[pl.BlockSpec(memory_space=pltpu.HBM)] * 3,
+        scratch_shapes=[sems(3, L)],
+        compiler_params=pltpu.CompilerParams(vmem_limit_bytes=8 * 1024 * 1024),
+    )(*outs)
 
 
 def solution(mesh):

time: 74.2 us -> 69.7 us (0.939)
  Pallas kernels: 68.4 us -> 64.1 us
    pallas_call x1, Pallas kernels: 68.4 us -> 61.3 us  [on_device(): pl.pallas_call(functools.partial(kernel, nt, ns, L, R, C), out_shape=[jax...]
    pallas_call x0 -> x1, Pallas kernels: none -> 2.75 us  [on_device(): pl.pallas_call(functools.partial(write_out, L), out_shape=[jax.ShapeDtype...]
    unnamed x5 -> x6, local copies, waits for them, and re-layouts: 4.99 us -> 4.77 us
where the time goes in v2:
time: 69.7 us; the launch traced here: 69.5 us
  Pallas kernels  64.1 us (92%)
  local copies, waits for them, and re-layouts  4.77 us (7%)
    pallas_call x1, Pallas kernels, on_device(): pl.pallas_call(functools.partial(kernel, nt, ns, L, R, C), out_shape=[jax...  61.3 us
    unnamed x6, local copies, waits for them, and re-layouts  4.77 us
    pallas_call x1, Pallas kernels, on_device(): pl.pallas_call(functools.partial(write_out, L), out_shape=[jax.ShapeDtype...  2.75 us

profile of v2, /device:TPU:0, one launch (start us, length us, event | category | flops | bytes accessed | tf_op | source)
XLA Modules:
  0.0 69.5 jit_solution(18021133376995541278)
XLA Ops:
  0.6 61.3 %shard_map.58 = (f32[4,64,2048]{2,1,0:T(8,128)}, f32[4,64,2048]{2,1,0:T(8,128)}, f32[4,64,2048]{2,1,0:T(8,128)}) custom-call(f32[4,64,2048]{2,1,0:T(8,128)} %src_h.1, f32[4,64,2048]{2,1,0:T(8,128)} %g_h.1, f32[4,64,2048]{2,1,0:T(8,128)} %f_h.1), custom_call_target="tpu_custom_call" | custom-call | tf_op jit(solution)/shard_map/pallas_call | solution.py:360
  62.0 0.0 copy-start
  62.0 1.6 %copy-done = f32[4,64,2048]{2,1,0:T(8,128)S(1)} copy-done((f32[4,64,2048]{2,1,0:T(8,128)S(1)}, f32[4,64,2048]{2,1,0:T(8,128)}, u32[]{:S(2)}) %copy-start) | copy-done | bytes 2097176
  63.5 0.0 copy-start.1
  63.6 1.6 %copy-done.1 = f32[4,64,2048]{2,1,0:T(8,128)S(1)} copy-done((f32[4,64,2048]{2,1,0:T(8,128)S(1)}, f32[4,64,2048]{2,1,0:T(8,128)}, u32[]{:S(2)}) %copy-start.1) | copy-done | bytes 2097176
  65.1 0.0 copy-start.2
  65.1 1.6 %copy-done.2 = f32[4,64,2048]{2,1,0:T(8,128)S(1)} copy-done((f32[4,64,2048]{2,1,0:T(8,128)S(1)}, f32[4,64,2048]{2,1,0:T(8,128)}, u32[]{:S(2)}) %copy-start.2) | copy-done | bytes 2097176
  66.7 2.7 %shard_map.59 = (f32[4,64,2048]{2,1,0:T(8,128)}, f32[4,64,2048]{2,1,0:T(8,128)}, f32[4,64,2048]{2,1,0:T(8,128)}) custom-call(f32[4,64,2048]{2,1,0:T(8,128)S(1)} %copy-done, f32[4,64,2048]{2,1,0:T(8,128)S(1)} %copy-done.1, f32[4,64,2048]{2,1,0:T(8,128)S(1)} %copy-done.2), custom_call_target="tpu_custom_call" | custom-call | tf_op jit(solution)/shard_map/pallas_call | solution.py:375
Async XLA Ops:
  62.0 1.6 %copy-start = (f32[4,64,2048]{2,1,0:T(8,128)S(1)}, f32[4,64,2048]{2,1,0:T(8,128)}, u32[]{:S(2)}) copy-start(f32[4,64,2048]{2,1,0:T(8,128)} %get-tuple-element.6.a) | copy-start | bytes 6291460
  63.5 1.6 %copy-start.1 = (f32[4,64,2048]{2,1,0:T(8,128)S(1)}, f32[4,64,2048]{2,1,0:T(8,128)}, u32[]{:S(2)}) copy-start(f32[4,64,2048]{2,1,0:T(8,128)} %get-tuple-element.7.b) | copy-start | bytes 6291460
  65.1 1.6 %copy-start.2 = (f32[4,64,2048]{2,1,0:T(8,128)S(1)}, f32[4,64,2048]{2,1,0:T(8,128)}, u32[]{:S(2)}) copy-start(f32[4,64,2048]{2,1,0:T(8,128)} %get-tuple-element.8.c) | copy-start | bytes 6291460

commit v3 on v2

--- a/solution.py
+++ b/solution.py
@@ -181,7 +181,6 @@
 
     each(1, body_c)
     send_c = to_prev(c0, cN, 2)
-    send_c.start()
 
     def body_r(base):
         def body(t, i, c):
@@ -202,6 +201,7 @@
 
     each(1, body_d)
     x2b = halo(bp, TILE, bp, last, 1, 2)
+    send_c.start()
     norm = each(last - 1, body_r(1), zero)
     x3c = halo(rp, TILE, rp, 1, last - 1, 8)
     x2b()
@@ -219,9 +219,7 @@
     each(1, body_e)
     send_r = [to_next(carr.at[pl.ds(i * TILE, TILE)], rin.at[pl.ds(i * TILE, TILE)], css.at[i], crs.at[i])
               for i in range(NB)]
-    early = NB * 5 // 8
-    for i in range(early):
-        send_r[i].start()
+    early = NB * 4 // 8
 
     def body_f(base):
         def body(t, i, c):
@@ -262,6 +260,8 @@
         im[0, rows(i), :] = rp[0, rows(i, TILE), :] - k
         return c
 
+    for i in range(early):
+        send_r[i].start()
     send_c.wait_recv()
 
     def body_h(_, i, c):
@@ -370,8 +370,8 @@
             sems(NB), sems(NB), sems(ns), sems(ns), sems(nt), sems(nt),
         ],
         compiler_params=pltpu.CompilerParams(
-            collective_id=0, has_side_effects=True, vmem_limit_bytes=57 * 1024 * 1024),
-    )(source, guess, field)
+            collective_id=0, has_side_effects=True, vmem_limit_bytes=40 * 1024 * 1024),
+    )(*(pltpu.with_memory_space_constraint(x, pltpu.HBM) for x in (source, guess, field)))
     return pl.pallas_call(
         functools.partial(write_out, L),
         out_shape=[jax.ShapeDtypeStruct((L, R, C), f32)] * 3,

time: 69.7 us -> 61.4 us (0.88)
  local copies, waits for them, and re-layouts: 4.77 us -> 0 us
  Pallas kernels: 64.1 us -> 60.6 us
    unnamed x6 -> x0, local copies, waits for them, and re-layouts: 4.77 us -> none
    pallas_call x1, Pallas kernels: 61.3 us -> 57.8 us  [on_device(): pl.pallas_call(functools.partial(kernel, nt, ns, L, R, C), out_shape=[jax...]
where the time goes in v3:
time: 61.4 us; the launch traced here: 61.2 us
  Pallas kernels  60.6 us (99%)
  between operations  0.64 us (1%)
    pallas_call x1, Pallas kernels, on_device(): pl.pallas_call(functools.partial(kernel, nt, ns, L, R, C), out_shape=[jax...  57.8 us
    pallas_call x1, Pallas kernels, on_device(): pl.pallas_call(functools.partial(write_out, L), out_shape=[jax.ShapeDtype...  2.75 us

profile of v3, /device:TPU:0, one launch (start us, length us, event | category | flops | bytes accessed | tf_op | source)
XLA Modules:
  0.0 61.2 jit_solution(1843770477549725707)
XLA Ops:
  0.6 57.8 %shard_map.58 = (f32[4,64,2048]{2,1,0:T(8,128)S(1)}, f32[4,64,2048]{2,1,0:T(8,128)S(1)}, f32[4,64,2048]{2,1,0:T(8,128)S(1)}) custom-call(f32[4,64,2048]{2,1,0:T(8,128)} %src_h.1, f32[4,64,2048]{2,1,0:T(8,128)} %g_h.1, f32[4,64,2048]{2,1,0:T(8,128)} %f_h.1), custom_call_target="tpu_custom_call" | custom-call | tf_op jit(solution)/shard_map/pallas_call | solution.py:360
  58.5 2.8 %shard_map.59 = (f32[4,64,2048]{2,1,0:T(8,128)}, f32[4,64,2048]{2,1,0:T(8,128)}, f32[4,64,2048]{2,1,0:T(8,128)}) custom-call(f32[4,64,2048]{2,1,0:T(8,128)S(1)} %get-tuple-element.6.a, f32[4,64,2048]{2,1,0:T(8,128)S(1)} %get-tuple-element.7.b, f32[4,64,2048]{2,1,0:T(8,128)S(1)} %get-tuple-element.8.c), custom_call_target="tpu_custom_call" | custom-call | tf_op jit(solution)/shard_map/pallas_call | solution.py:375

commit v4 on v3

--- a/solution.py
+++ b/solution.py
@@ -219,7 +219,7 @@
     each(1, body_e)
     send_r = [to_next(carr.at[pl.ds(i * TILE, TILE)], rin.at[pl.ds(i * TILE, TILE)], css.at[i], crs.at[i])
               for i in range(NB)]
-    early = NB * 4 // 8
+    early, mid = NB * 2 // 8, NB * 5 // 8
 
     def body_f(base):
         def body(t, i, c):
@@ -263,6 +263,8 @@
     for i in range(early):
         send_r[i].start()
     send_c.wait_recv()
+    for i in range(early, mid):
+        send_r[i].start()
 
     def body_h(_, i, c):
         carried = carr[rows(i), :]
@@ -302,7 +304,7 @@
     acc[1] = total
     tmg[tm] = total
     sum2, wait2 = gather(1, tmg, 0, tm, nt, s2s, s2r)
-    for i in range(early, NB):
+    for i in range(mid, NB):
         send_r[i].start()
     x4a()
     each(1, body_y0)

time: 61.4 us -> 60.2 us (0.980)
  Pallas kernels: 60.6 us -> 59.4 us
    pallas_call x1, Pallas kernels: 57.8 us -> 56.6 us  [on_device(): pl.pallas_call(functools.partial(kernel, nt, ns, L, R, C), out_shape=[jax...]
where the time goes in v4:
time: 60.2 us; the launch traced here: 60 us
  Pallas kernels  59.4 us (99%)
  between operations  0.64 us (1%)
    pallas_call x1, Pallas kernels, on_device(): pl.pallas_call(functools.partial(kernel, nt, ns, L, R, C), out_shape=[jax...  56.6 us
    pallas_call x1, Pallas kernels, on_device(): pl.pallas_call(functools.partial(write_out, L), out_shape=[jax.ShapeDtype...  2.75 us

profile of v4, /device:TPU:0, one launch (start us, length us, event | category | flops | bytes accessed | tf_op | source)
XLA Modules:
  0.0 60.0 jit_solution(1433147944602516923)
XLA Ops:
  0.6 56.6 %shard_map.58 = (f32[4,64,2048]{2,1,0:T(8,128)S(1)}, f32[4,64,2048]{2,1,0:T(8,128)S(1)}, f32[4,64,2048]{2,1,0:T(8,128)S(1)}) custom-call(f32[4,64,2048]{2,1,0:T(8,128)} %src_h.1, f32[4,64,2048]{2,1,0:T(8,128)} %g_h.1, f32[4,64,2048]{2,1,0:T(8,128)} %f_h.1), custom_call_target="tpu_custom_call" | custom-call | tf_op jit(solution)/shard_map/pallas_call | solution.py:362
  57.2 2.8 %shard_map.59 = (f32[4,64,2048]{2,1,0:T(8,128)}, f32[4,64,2048]{2,1,0:T(8,128)}, f32[4,64,2048]{2,1,0:T(8,128)}) custom-call(f32[4,64,2048]{2,1,0:T(8,128)S(1)} %get-tuple-element.6.a, f32[4,64,2048]{2,1,0:T(8,128)S(1)} %get-tuple-element.7.b, f32[4,64,2048]{2,1,0:T(8,128)S(1)} %get-tuple-element.8.c), custom_call_target="tpu_custom_call" | custom-call | tf_op jit(solution)/shard_map/pallas_call | solution.py:377
